TPU v7x, 512 devices: a whole 4x4x16 slice. The times are simulated.
512 devices in a mesh: ctx: 64 (over z_lo, x, core), tp: 8 (over y, z_hi).
Axes of the slice: x: 4, y: 4, z: 16 (z_hi: 2, z_lo: 8; z = z_hi * 8 + z_lo), core: 2. Of those that a mesh axis runs over, the one named last changes fastest.
Arguments:
- hidden_x: bfloat16 [8192, 8192], P('ctx', 'tp'), may hold values from -100 to 100, as said below
- norm_gain: float32 [8192], replicated, may hold values from 0.1 to 1.9
- key_projection: bfloat16 [8192, 1024], P('ctx', 'tp'), may hold values from -0.0625 to 0.0625
- value_projection: bfloat16 [8192, 1024], P('ctx', 'tp'), may hold values from -0.0625 to 0.0625
- queries: bfloat16 [8192, 8192], P('ctx', 'tp'), may hold values from -160 to 160
- span_pair: int32 [64], P('ctx'), may hold values from 0 to 63, each once
- doc_lengths: int32 [12], replicated, may hold values from 1 to 2048, 8192 in all
Outputs:
- attended: bfloat16 [8192, 8192], P('ctx', 'tp')
Inputs may be any that keep to these rules, and one draw needn't show every extreme that they name: `hidden_x`: hidden states of tokens and features of different scales. `span_pair`: each pair index is held by exactly one index of ctx. `doc_lengths`: they sum to 8192; the longest has 2048 tokens.
All inputs are finite; a program needn't handle non-finite values.
Results may differ from a plain program's by a relative error of at most 0.0078.
Values may be sent and summed in bfloat16 or wider, within the bound.
A program may use at most 128 MiB of HBM per device.

v0:
```python
import math

import jax
import jax.numpy as jnp
from jax import lax
from jax.sharding import PartitionSpec as P

HEAD_SIZE = 128


ROPE_BASE = 500000.0
EPSILON = 1e-05
NEG_BIG = -1e30


def rotate_heads(raw, positions, head_dim):
    tokens_here = raw.shape[0]
    heads_here = raw.shape[1] // head_dim
    half_dim = head_dim // 2
    split_heads = raw.reshape(tokens_here, heads_here, head_dim)
    exponents = jnp.arange(half_dim, dtype=jnp.float32) * (2.0 / head_dim)
    inverse = jnp.power(jnp.float32(ROPE_BASE), -exponents)
    angles = positions.astype(jnp.float32)[:, None] * inverse[None, :]
    cosine = jnp.cos(angles)[:, None, :]
    sine_part = jnp.sin(angles)[:, None, :]
    first_half = split_heads[..., :half_dim]
    second_half = split_heads[..., half_dim:]
    turned = jnp.concatenate(
        [
            first_half * cosine - second_half * sine_part,
            second_half * cosine + first_half * sine_part,
        ],
        axis=-1,
    )
    return turned.reshape(tokens_here, heads_here * head_dim)


def place_tokens(pair_of_token, offsets, half_rows, span_total):
    early = pair_of_token * half_rows + offsets
    late = (span_total - 1 - pair_of_token) * half_rows + offsets - half_rows
    return jnp.where(offsets < half_rows, early, late)


def document_of(positions, doc_ends):
    return jnp.sum((positions[:, None] >= doc_ends[None, :]).astype(jnp.int32), axis=1)


def normalize(hidden_x, norm_gain):
    widened = hidden_x.astype(jnp.float32)
    mean_square = jnp.mean(widened * widened, axis=-1, keepdims=True)
    return (widened * lax.rsqrt(mean_square + EPSILON) * norm_gain).astype(jnp.bfloat16)


def shards(hidden_x, norm_gain, key_projection, value_projection, queries, span_pair, doc_lengths):
    context_count = lax.axis_size("ctx")
    tok_rows = hidden_x.shape[0]
    half_rows = tok_rows // 2
    sequence_rows = tok_rows * context_count
    head_dim = HEAD_SIZE
    pair_list = lax.all_gather(span_pair, "ctx", axis=0, tiled=True)
    whole_x = lax.all_gather(hidden_x, "tp", axis=1, tiled=True)
    normed = normalize(whole_x, norm_gain)
    key_width = key_projection.shape[1]
    key_raw = jnp.dot(
        normed,
        lax.all_gather(key_projection, "ctx", axis=0, tiled=True),
        preferred_element_type=jnp.float32,
    )
    value_raw = jnp.dot(
        normed,
        lax.all_gather(value_projection, "ctx", axis=0, tiled=True),
        preferred_element_type=jnp.float32,
    )
    offsets = jnp.arange(tok_rows, dtype=jnp.int32)
    own_positions = place_tokens(span_pair[0], offsets, half_rows, 2 * context_count)
    doc_ends = jnp.cumsum(doc_lengths)
    own_documents = document_of(own_positions, doc_ends)
    rows_of_key = rotate_heads(key_raw, own_positions, head_dim).astype(jnp.bfloat16)
    rows_of_value = value_raw.astype(jnp.bfloat16)
    local_heads = key_width // head_dim
    group_width = queries.shape[1] // head_dim // local_heads
    query_count = tok_rows * group_width
    query_rows = (
        queries.reshape(tok_rows, local_heads, group_width, head_dim)
        .transpose(1, 0, 2, 3)
        .reshape(local_heads, query_count, head_dim)
    )
    row_positions = jnp.repeat(own_positions, group_width)
    row_documents = jnp.repeat(own_documents, group_width)
    context_ids = jnp.arange(context_count, dtype=jnp.int32)
    scale_factor = HEAD_SIZE ** (-0.5)

    def key_places(first_row, row_count):
        token_ids = first_row + jnp.arange(row_count, dtype=jnp.int32)
        owners = token_ids // tok_rows
        chosen = jnp.sum(
            jnp.where(owners[:, None] == context_ids[None, :], pair_list[None, :], 0), axis=1
        )
        places = place_tokens(chosen, token_ids % tok_rows, half_rows, 2 * context_count)
        return (places, document_of(places, doc_ends))

    def attend(running, key_block, value_block, first_row):
        row_count = key_block.shape[0]
        places, key_documents = key_places(first_row, row_count)
        allowed = (key_documents[None, :] == row_documents[:, None]) & (
            places[None, :] <= row_positions[:, None]
        )
        top_now, total_now, acc_now = running
        heads_of_key = key_block.reshape(row_count, local_heads, head_dim)
        heads_of_value = value_block.reshape(row_count, local_heads, head_dim)
        scores = (
            jnp.einsum("hrd,nhd->hrn", query_rows, heads_of_key, preferred_element_type=jnp.float32)
            * scale_factor
        )
        scores = jnp.where(allowed[None], scores, NEG_BIG)
        top_next = jnp.maximum(top_now, jnp.max(scores, axis=2))
        shrink = jnp.exp(top_now - top_next)
        exp_scores = jnp.where(allowed[None], jnp.exp(scores - top_next[..., None]), 0.0)
        total_next = total_now * shrink + jnp.sum(exp_scores, axis=2)
        rounded = exp_scores.astype(jnp.bfloat16)
        acc_next = acc_now * shrink[..., None] + jnp.einsum(
            "hrn,nhd->hrd", rounded, heads_of_value, preferred_element_type=jnp.float32
        )
        return (top_next, total_next, acc_next)

    initial = (
        jnp.full((local_heads, query_count), NEG_BIG, jnp.float32),
        jnp.zeros((local_heads, query_count), jnp.float32),
        jnp.zeros((local_heads, query_count, head_dim), jnp.float32),
    )
    all_keys, all_values = (
        lax.all_gather(rows_of_key, "ctx", axis=0, tiled=True),
        lax.all_gather(rows_of_value, "ctx", axis=0, tiled=True),
    )
    block_rows = math.gcd(sequence_rows, 512)

    def step_block(block_index, running):
        first_row = block_index * block_rows
        key_block = lax.dynamic_slice_in_dim(all_keys, first_row, block_rows, 0)
        value_block = lax.dynamic_slice_in_dim(all_values, first_row, block_rows, 0)
        return attend(running, key_block, value_block, first_row)

    final_state = lax.fori_loop(0, sequence_rows // block_rows, step_block, initial)
    top_final, total_final, acc_final = final_state
    attended = (acc_final / total_final[..., None]).astype(jnp.bfloat16)
    return (
        attended.reshape(local_heads, tok_rows, group_width, head_dim)
        .transpose(1, 0, 2, 3)
        .reshape(tok_rows, local_heads * group_width * head_dim)
    )


def solution(mesh):
    placed = (P("ctx", "tp"), P(), P("ctx", "tp"), P("ctx", "tp"), P("ctx", "tp"), P("ctx"), P())
    return jax.shard_map(
        shards, mesh=mesh, in_specs=placed, out_specs=P("ctx", "tp"), check_vma=False
    )
```

profile of v0, /device:TPU:1, one launch (start us, length us, event | category | flops | bytes accessed | tf_op | source)
XLA Modules:
  0.0 689.2 jit_solution(12712746274023242138)
XLA Ops:
  8.8 123.9 %all-gather.7.cloned.1.call-done = bf16[128,8192]{1,0:T(8,128)(2,1)} async-done(((bf16[128,1024]{1,0:T(8,128)(2,1)}), bf16[128,8192]{1,0:T(8,128)(2,1)}) %all-gather.7.cloned.1.call-update) | async-done | bytes 2097168 | tf_op jit(solution)/shard_map/all_gather | solution.py:61
  132.7 2.2 fusion.34
  134.9 115.5 %all-gather.11.cloned.1.call-done = bf16[8192,128]{1,0:T(8,128)(2,1)} async-done(((bf16[128,128]{1,0:T(8,128)(2,1)}), bf16[8192,128]{1,0:T(8,128)(2,1)}) %all-gather.11.cloned.1.call-update) | async-done | bytes 2097168 | tf_op jit(solution)/shard_map/all_gather | solution.py:71
  250.4 3.0 convolution_convert_fusion
  254.2 114.8 %all-gather.9.cloned.1.call-done = bf16[8192,128]{1,0:T(8,128)(2,1)} async-done(((bf16[128,128]{1,0:T(8,128)(2,1)}), bf16[8192,128]{1,0:T(8,128)(2,1)}) %all-gather.9.cloned.1.call-update) | async-done | bytes 2097168 | tf_op jit(solution)/shard_map/all_gather | solution.py:66
  369.0 2.7 convolution_bitcast_fusion.1
  374.8 13.5 %all-reduce = s32[64]{0:T(128)S(1)} all-reduce(s32[64]{0:T(128)S(1)} %dynamic-update-slice), channel_id=1, replica_groups=mesh['ctx'=64,'tp'=8] {'ctx'}, use_global_device_ids=true, to_apply=%add | all-reduce | flops 64 | bytes 512
  388.4 99.0 %all-gather.13.cloned.1.call-done = bf16[8192,128]{1,0:T(8,128)(2,1)} async-done(((bf16[128,128]{1,0:T(8,128)(2,1)}), bf16[8192,128]{1,0:T(8,128)(2,1)}) %all-gather.13.cloned.1.call-update) | async-done | bytes 2097168 | tf_op jit(solution)/shard_map/all_gather | solution.py:133
  487.5 115.9 %all-gather.15.cloned.1.call-done = bf16[8192,1,128]{0,2,1:T(8,128)(2,1)} async-done(((bf16[128,1,128]{0,2,1:T(8,128)(2,1)}), bf16[8192,1,128]{0,2,1:T(8,128)(2,1)}) %all-gather.15.cloned.1.call-update) | async-done | bytes 2097168 | tf_op jit(solution)/shard_map/all_gather | solution.py:132
  603.4 78.2 %while.20 = (s32[]{:T(128)}, f32[1,1024]{1,0:T(1,128)S(1)}, f32[1,1024]{1,0:T(1,128)S(1)}, f32[1,1024,128]{2,1,0:T(8,128)S(1)}, s32[64]{0:T(128)S(1)}, /*index=5...) while((s32[]{:T(128)}, f32[1,1024]{1,0:T(1,128)S(1)}, ...), condition=%wide.region_8.9_spmd.clone, body=%wide.region_3.8_spmd.clone.sunk | while | flops 280502272 | bytes 8007183 | solution.py:143
  606.4 1.9 fusion.63
  608.9 1.6 fusion.59
  611.3 1.9 fusion.63
  616.1 1.9 fusion.63
  618.6 1.6 fusion.59
  621.0 1.9 fusion.63
  625.9 1.9 fusion.63
  628.4 1.6 fusion.59
  630.8 1.9 fusion.63
  635.7 1.9 fusion.63
  638.2 1.6 fusion.59
  640.6 1.9 fusion.63
  645.5 1.9 fusion.63
  648.0 1.6 fusion.59
  650.4 1.9 fusion.63
  655.3 1.9 fusion.63
  657.7 1.6 fusion.59
  660.1 1.9 fusion.63
  665.0 1.9 fusion.63
  669.9 1.9 fusion.63
  674.8 1.9 fusion.63
  679.7 1.9 fusion.63
  (236 shorter events, 43.7 us)
Async XLA Ops:
  6.5 243.9 %copy-start.2 = (f32[8192]{0:T(1024)S(1)}, f32[8192]{0:T(1024)}, u32[]{:S(2)}) copy-start(f32[8192]{0:T(1024)} %param.10) | copy-start | bytes 98308
  6.5 126.1 %all-gather.7.cloned.1.call-start = ((), (), s32[]{:S(2)}) async-start(), calls=%async_computation | async-start | bytes 2359296 | tf_op jit(solution)/shard_map/all_gather | solution.py:61
  7.3 243.1 %all-gather.11.cloned.1.call-start = ((), (), s32[]{:S(2)}) async-start(), calls=%async_computation.2 | async-start | bytes 2129920 | tf_op jit(solution)/shard_map/all_gather | solution.py:71
  8.0 361.0 %all-gather.9.cloned.1.call-start = ((), (), s32[]{:S(2)}) async-start(), calls=%async_computation.1 | async-start | bytes 2129920 | tf_op jit(solution)/shard_map/all_gather | solution.py:66
  8.7 478.7 %all-gather.13.cloned.1.call-start = ((), (), s32[]{:S(2)}) async-start(), calls=%async_computation.3 | async-start | bytes 2129920 | tf_op jit(solution)/shard_map/all_gather | solution.py:133
  132.7 117.7 %copy-start = (bf16[128,8192]{1,0:T(8,128)(2,1)S(1)}, bf16[128,8192]{1,0:T(8,128)(2,1)}, u32[]{:S(2)}) copy-start(bf16[128,8192]{1,0:T(8,128)(2,1)} %all-gather.7.cloned.1.call-done) | copy-start | bytes 6291460
  253.5 349.9 %all-gather.15.cloned.1.call-start = ((), (), s32[]{:S(2)}) async-start(), calls=%async_computation.4 | async-start | bytes 2129920 | tf_op jit(solution)/shard_map/all_gather | solution.py:132
  254.2 118.4 %copy-start.3 = (s32[12]{0:T(128)S(1)}, s32[12]{0:T(128)}, u32[]{:S(2)}) copy-start(s32[12]{0:T(128)} %param.15) | copy-start | bytes 148
  254.2 118.6 %copy-start.1 = (bf16[128,1024]{1,0:T(8,128)(2,1)S(1)}, bf16[128,1024]{1,0:T(8,128)(2,1)}, u32[]{:S(2)}) copy-start(bf16[128,1024]{1,0:T(8,128)(2,1)} %param.13) | copy-start | bytes 786436
Sparse Core Ops, SparseCore 0:
  10.6 122.0 all-gather.6
  134.8 115.5 all-gather.10
  252.5 116.4 all-gather.8
  371.0 116.4 all-gather.12
  489.4 113.9 all-gather.14
where the time goes:
time: 690 us; the launch traced here: 689 us
  waiting for transfers between devices  571 us (83%)
  matrix products  61.4 us (9%)
  other arithmetic  19.3 us (3%)
  between operations  13.9 us (2%)
  blocking collectives  13.5 us (2%)
  local copies, waits for them, and re-layouts  8.41 us (1%)
    all_gather x1, waiting for transfers between devices, shards(): whole_x = lax.all_gather(hidden_x, 'tp', axis=1, tiled=True)  124 us
    all_gather x1, waiting for transfers between devices, shards(): lax.all_gather(rows_of_key, 'ctx', axis=0, tiled=True)  116 us
    all_gather x1, waiting for transfers between devices, shards(): lax.all_gather(value_projection, 'ctx', axis=0, tiled=True)  115 us
    all_gather x1, waiting for transfers between devices, shards(): lax.all_gather(key_projection, 'ctx', axis=0, tiled=True)  115 us
    all_gather x1, waiting for transfers between devices, shards(): lax.all_gather(rows_of_value, 'ctx', axis=0, tiled=True)  99 us
    dot_general x16, matrix products, attend(): jnp.einsum('hrn,nhd->hrd', rounded, heads_of_value, preferred_element_typ...  30 us
    dot_general x16, matrix products, attend(): jnp.einsum('hrd,nhd->hrn', query_rows, heads_of_key, preferred_element_ty...  25.7 us
  transfers between devices with their start and end apart: 5, of which 5 were waited for; matrix products, arithmetic and copies ran while one was open for 2% of the time, Pallas kernels for 0%

commit v1 on v0

v1 whole, which is shorter than its diff:
```python
import functools
import math

import jax
import jax.numpy as jnp
import numpy as np
from jax import lax
from jax.experimental import pallas as pl
from jax.experimental.pallas import tpu as pltpu
from jax.sharding import PartitionSpec as P

HEAD = 128
ROPE_BASE = 500000.0
EPSILON = 1e-05
NEG = -1e30
MESH = pl.DeviceIdType.MESH
NZ, NX, NY = 8, 4, 4
NCTX = NZ * NX * 2
HALF = 64
EXT = 16
VMEM_LIMIT = 60 * 1024 * 1024
HUB = {0: (4, 1), 1: (2,), 2: (3,), 4: (6, 5), 6: (7,)}
LINE = {i: (i + 1,) for i in range(NZ - 1)}
SPREAD = (
    "z0", "z1", "z4", "z2", "x0", "z5", "z3", "x1", "z6", "a0", "x4", "z7", "x2", "a1", "x5", "a4", "x3", "a2", "x6",
    "a5", "x7", "a3", "a6", "a7",
)
REACHES = (1, 2, 4)


def block_id(z, x, k):
    return z * (NX * 2) + x * 2 + k


class Place:
    def __init__(self):
        self.ctx = lax.axis_index("ctx")
        self.tp = lax.axis_index("tp")
        self.z = self.ctx // (NX * 2)
        self.x = (self.ctx // 2) % NX
        self.k = self.ctx % 2
        self.y = self.tp // 2
        self.h = self.tp % 2

    def ctx_neighbour(self, what):
        if isinstance(what, int):
            return block_id(self.z + what, self.x, self.k)
        if what == "right":
            return block_id(self.z, (self.x + 1) % NX, self.k)
        if what == "left":
            return block_id(self.z, (self.x + NX - 1) % NX, self.k)
        return block_id(self.z, self.x, 1 - self.k)


def copy_to(src, dst, send, recv, device):
    return pltpu.make_async_remote_copy(
        src_ref=src, dst_ref=dst, send_sem=send, recv_sem=recv, device_id=device, device_id_type=MESH
    )


class CtxGather:
    def __init__(self, place, tree, bufs, send, recv):
        self.p, self.tree, self.bufs, self.send, self.recv = place, tree, bufs, send, recv

    N_SEND = 74

    def copy(self, array, block, slot, way):
        ref = self.bufs[array].at[block]
        return copy_to(
            ref,
            ref,
            self.send.at[array, slot],
            self.recv.at[array, block],
            {"ctx": self.p.ctx_neighbour(way)},
        )

    def arrived(self, array, block):
        self.copy(array, block, 0, "core").wait_recv()

    def spread(self, array, zb):
        p = self.p
        own = block_id(zb, p.x, p.k)
        self.copy(array, own, 18 + zb, "right").start()
        self.copy(array, own, 26 + zb, "left").start()
        self.copy(array, own, 42 + zb * NX + p.x, "core").start()

    def within(self, z):
        return jnp.logical_and(z >= 0, z <= NZ - 1)

    def onward(self, distance, sign, what):
        p = self.p
        zb = p.z - sign * distance
        for n, child in enumerate(self.tree.get(distance, ())):
            reach = sign * (child - distance)
            slot = 16 + n if distance == 0 and sign < 0 else 8 * n + zb

            @pl.when(self.within(p.z + reach))
            def _(reach=reach, slot=slot):
                for a in range(2):
                    what(a, block_id(zb, p.x, p.k), slot, reach)

    def column(self, distance):
        p = self.p

        def send(a, block, slot, reach):
            self.copy(a, block, slot, reach).start()

        if distance == 0:
            self.onward(0, 1, send)
            self.onward(0, -1, send)
            for a in range(2):
                self.spread(a, p.z)
            return
        for sign in (1, -1):

            @pl.when(self.within(p.z - sign * distance))
            def _(sign=sign):
                zb = p.z - sign * distance
                for a in range(2):
                    self.arrived(a, block_id(zb, p.x, p.k))
                self.onward(distance, sign, send)
                for a in range(2):
                    self.spread(a, zb)

    def act(self, action):
        what, distance = action[0], int(action[1:])
        if what == "z":
            self.column(distance)
        else:
            self.each(distance, self.from_side if what == "x" else self.from_across)

    def each(self, distance, what):
        p = self.p

        @pl.when(p.z - distance >= 0)
        def _():
            what(p.z - distance)

        if distance:

            @pl.when(p.z + distance <= NZ - 1)
            def _():
                what(p.z + distance)

    def from_side(self, zb):
        p = self.p
        left, right = (p.x + NX - 1) % NX, (p.x + 1) % NX
        for x, relayed, way in ((left, 0, "right"), (right, 1, "left")):
            block = block_id(zb, x, p.k)
            for a in range(2):
                self.arrived(a, block)
                if a == relayed:
                    self.copy(a, block, 34 + zb, way).start()
                self.copy(a, block, 42 + zb * NX + x, "core").start()

    def from_across(self, zb):
        p = self.p
        x = (p.x + 2) % NX
        block = block_id(zb, x, p.k)
        for a in range(2):
            self.arrived(a, block)
            self.copy(a, block, 42 + zb * NX + x, "core").start()

    def other_core(self, landed=None):
        p = self.p

        @pl.loop(0, NZ * NX)
        def _(i):
            for a in range(2):
                self.arrived(a, i * 2 + 1 - p.k)
            if landed is not None:
                landed(i)

    def drain(self):
        p = self.p

        @pl.loop(0, NZ)
        def _(zb):
            own = block_id(zb, p.x, p.k)
            for a in range(2):
                self.copy(a, own, 18 + zb, "right").wait_send()
                self.copy(a, own, 26 + zb, "left").wait_send()
                self.copy(a, own, 34 + zb, "left").wait_send()
                for x in range(NX):
                    self.copy(a, own, 42 + zb * NX + x, "core").wait_send()

        def sent(a, block, slot, reach):
            self.copy(a, block, slot, reach).wait_send()

        for distance in self.tree:
            for sign in (1, -1):

                @pl.when(self.within(p.z - sign * distance))
                def _(distance=distance, sign=sign):
                    self.onward(distance, sign, sent)


CHUNKS = 8


class FeatureGather:
    N_SEND = 7 * CHUNKS

    def __init__(self, place, x_ref, buf, send, recv):
        self.p, self.x_ref, self.buf, self.send, self.recv = place, x_ref, buf, send, recv
        self.rows = x_ref.shape[0] // CHUNKS
        p = place
        self.across_z = {"tp": p.y * 2 + 1 - p.h}
        self.right = {"tp": ((p.y + 1) % NY) * 2 + p.h}
        self.left = {"tp": ((p.y + NY - 1) % NY) * 2 + p.h}

    def copy(self, slot, chunk, kind, device, own=False):
        part = pl.ds(chunk * self.rows, self.rows)
        src = self.x_ref.at[part] if own else self.buf.at[slot, part]
        return copy_to(
            src, self.buf.at[slot, part], self.send.at[kind * CHUNKS + chunk], self.recv.at[slot, chunk], device
        )

    def arrived(self, slot, chunk):
        self.copy(slot, chunk, 0, self.left).wait_recv()

    def slots(self, partner):
        p = self.p
        h = 1 - p.h if partner else p.h
        return [((p.y + step) % NY) * 2 + h for step in (0, NY - 1, 1, 2)]

    def act(self, action):
        what = {"y": self.start, "c": self.cross, "r": self.relay, "p": self.partner, "q": self.partner_relay}
        what[action[0]](int(action[1:]))

    def start(self, _):
        own = self.p.tp
        for i in range(CHUNKS):
            self.copy(own, i, 1, self.right, True).start()
            self.copy(own, CHUNKS - 1 - i, 2, self.left, True).start()

    def cross(self, i):
        self.copy(self.p.tp, i, 0, self.across_z, True).start()

    def relay(self, i):
        _, left, right, _ = self.slots(False)
        last = CHUNKS - 1 - i
        self.arrived(left, i)
        if i < CHUNKS // 2:
            self.copy(left, i, 3, self.right).start()
        self.arrived(right, last)
        if i < CHUNKS // 2:
            self.copy(right, last, 3, self.left).start()

    def partner(self, i):
        slot = self.slots(True)[0]
        self.arrived(slot, i)
        self.copy(slot, i, 4, self.right).start()
        self.copy(slot, i, 5, self.left).start()

    def partner_relay(self, i):
        _, left, right, _ = self.slots(True)
        self.arrived(left, i)
        if i % 2 == 0:
            self.copy(left, i, 6, self.right).start()
        self.arrived(right, i)
        if i % 2 == 1:
            self.copy(right, i, 6, self.left).start()

    def across(self, i):
        for partner in (False, True):
            self.arrived(self.slots(partner)[3], i)

    def drain(self):
        for kind in range(7):
            for i in range(CHUNKS):
                self.copy(self.p.tp, i, kind, self.left, True).wait_send()


SCHEDULE = (
    "z0", "y0", "c0", "z1", "x0", "c1", "r0", "r1", "z2", "x1", "a0", "c2", "r2", "r3", "z3", "x2", "a1", "c3", "r4",
    "r5", "z4", "x3", "a2", "c4", "r6", "r7", "z5", "x4", "a3", "c5", "p0", "z6", "x5", "a4", "c6", "p1", "z7", "x6",
    "a5", "c7", "p2", "q0", "x7", "a6", "p3", "q1", "t", "p4", "q2", "n0", "a7", "p5", "q3", "n1", "o", "p6", "q4",
    "n2", "p7", "q5", "n3", "q6", "n4", "q7", "n5", "n6", "n7",
)


def greet(devices, optional):
    barrier = pltpu.get_barrier_semaphore()
    count = len(devices)
    for device in devices:
        pl.semaphore_signal(barrier, inc=1, device_id=device, device_id_type=MESH)
    for there, device in optional:

        @pl.when(there)
        def _(device=device):
            pl.semaphore_signal(barrier, inc=1, device_id=device, device_id_type=MESH)

        count = count + there.astype(jnp.int32)
    pl.semaphore_wait(barrier, count)


def ctx_partners(p):
    fixed = [{"ctx": p.ctx_neighbour(w)} for w in ("right", "left", "core")]
    optional = []
    for reach in REACHES:
        optional.append((p.z + reach <= NZ - 1, {"ctx": p.ctx_neighbour(reach)}))
        optional.append((p.z - reach >= 0, {"ctx": p.ctx_neighbour(-reach)}))
    return fixed, optional


def project_kernel(
    pair_ref, x_ref, gain_ref, wk_ref, wv_ref, freq_ref, keys_ref, values_ref, where_ref,
    xbuf, normed, wk_buf, wv_buf, turn, key_buf, value_buf, w_send, w_recv, x_send, x_recv, kv_send, kv_recv, local, store,
):
    p = Place()
    own = p.ctx
    rows, width = x_ref.shape
    half = rows // 2
    weights = CtxGather(p, LINE, (wk_buf, wv_buf), w_send, w_recv)
    features = FeatureGather(p, x_ref, xbuf, x_send, x_recv)
    spread = CtxGather(p, HUB, (key_buf, value_buf), kv_send, kv_recv)
    copies = [
        pltpu.make_async_copy(wk_ref, wk_buf.at[own, pl.ds(0, 128)], local.at[0]),
        pltpu.make_async_copy(wv_ref, wv_buf.at[own], local.at[1]),
        pltpu.make_async_copy(x_ref, xbuf.at[p.tp], local.at[2]),
    ]
    for c in copies:
        c.start()
    pair = pair_ref[0]
    wk_buf[own, pl.ds(128, EXT), :] = jnp.full((EXT, 128), pair.astype(jnp.float32), jnp.bfloat16)
    fixed, optional = ctx_partners(p)
    greet(fixed + [features.right, features.left, features.across_z], optional)
    for c in copies:
        c.wait()

    def normalize(chunk):
        part = pl.ds(chunk * features.rows, features.rows)
        squares = jnp.zeros((features.rows, HEAD), jnp.float32)
        for f in range(8):
            for i in range(width // HEAD):
                piece = xbuf[f, part, pl.ds(i * HEAD, HEAD)].astype(jnp.float32)
                squares = squares + piece * piece
        inverse = lax.rsqrt(jnp.sum(squares, axis=1, keepdims=True) / (8.0 * width) + EPSILON)
        for f in range(8):
            for i in range(width // HEAD):
                piece = xbuf[f, part, pl.ds(i * HEAD, HEAD)].astype(jnp.float32)
                gain = gain_ref[pl.ds(f * (width // HEAD) + i, 1), :]
                normed[f, part, pl.ds(i * HEAD, HEAD)] = (piece * inverse * gain).astype(jnp.bfloat16)

    token = lax.broadcasted_iota(jnp.int32, (rows, HEAD), 0)
    lane = lax.broadcasted_iota(jnp.int32, (rows, HEAD), 1)
    position = jnp.where(token < half, pair * half + token, (2 * NCTX - 1 - pair) * half + token - half)
    angle = position.astype(jnp.float32) * freq_ref[...]

    for action in SCHEDULE:
        if action[0] in "zxa":
            weights.act(action)
        elif action == "o":
            weights.other_core()
            held = jnp.max(wk_buf[:, pl.ds(128, EXT), :].astype(jnp.float32), axis=1)
            owner = lax.broadcasted_iota(jnp.int32, (NCTX, 128), 0).astype(jnp.float32)
            wanted = lax.broadcasted_iota(jnp.int32, (NCTX, 128), 1).astype(jnp.float32)
            where_ref[...] = jnp.sum(jnp.where(held == wanted, owner, 0.0), axis=0, keepdims=True).astype(jnp.int32)
        elif action == "t":
            turn[0] = jnp.cos(angle)
            turn[1] = jnp.where(lane < HEAD // 2, -jnp.sin(angle), jnp.sin(angle))
        elif action[0] == "n":
            features.across(int(action[1:]))
            normalize(int(action[1:]))
        else:
            features.act(action)

    keys = jnp.zeros((rows, HEAD), jnp.float32)
    values = jnp.zeros((rows, HEAD), jnp.float32)
    for f in range(8):
        wk = wk_buf[pl.ds(f * 8, 8), pl.ds(0, 128), :].reshape(width, HEAD)
        wv = wv_buf[pl.ds(f * 8, 8)].reshape(width, HEAD)
        keys = keys + jnp.dot(normed[f], wk, preferred_element_type=jnp.float32)
        values = values + jnp.dot(normed[f], wv, preferred_element_type=jnp.float32)
    key_buf[own] = (keys * turn[0] + pltpu.roll(keys, HEAD // 2, 1) * turn[1]).astype(jnp.bfloat16)
    value_buf[own] = values.astype(jnp.bfloat16)
    weights.drain()

    for action in SPREAD:
        spread.act(action)

    def stores(i):
        pair_of_blocks = pl.ds(i * 2, 2)
        return (
            pltpu.make_async_copy(key_buf.at[pair_of_blocks], keys_ref.at[pair_of_blocks], store.at[0, i]),
            pltpu.make_async_copy(value_buf.at[pair_of_blocks], values_ref.at[pair_of_blocks], store.at[1, i]),
        )

    def landed(i):
        for c in stores(i):
            c.start()

    spread.other_core(landed)
    features.drain()
    spread.drain()

    @pl.loop(0, NCTX // 2)
    def _(i):
        for c in stores(i):
            c.wait()


SPANS = 4
MOST_SPANS = 36


def attend_kernel(
    pair_ref, docs_ref, where_ref, q_ref, keys_ref, values_ref, out_ref, k_buf, v_buf, all_scores, highest, total, acc, sem
):
    group = q_ref.shape[1] // HEAD
    rows = HALF * group
    wide = SPANS * HALF
    factor = HEAD ** (-0.5) * math.log2(math.e)
    ends = []
    end = jnp.int32(0)
    for d in range(docs_ref.shape[0]):
        end = end + docs_ref[d]
        ends.append(end)
    pair = pair_ref[0]

    def start_of(position):
        first = jnp.zeros_like(position)
        for e in ends:
            first = jnp.where(position >= e, e, first)
        return first

    spans = [pair, 2 * NCTX - 1 - pair]
    firsts = [start_of(span * HALF) // HALF for span in spans]
    groups = [(span - first) // SPANS + 1 for span, first in zip(spans, firsts)]

    def fetches(part, i):
        j = jnp.minimum(firsts[part] + i, spans[part])
        late = j >= NCTX
        holder = where_ref[0, jnp.where(late, 2 * NCTX - 1 - j, j)]
        source = pl.ds(pl.multiple_of(jnp.where(late, HALF, 0), HALF), HALF)
        target = pl.ds(pl.multiple_of(i * HALF, HALF), HALF)
        return (
            pltpu.make_async_copy(keys_ref.at[holder, source], k_buf.at[part, target], sem.at[0, part, i]),
            pltpu.make_async_copy(values_ref.at[holder, source], v_buf.at[part, target], sem.at[1, part, i]),
        )

    for part in range(2):

        @pl.loop(0, groups[part] * SPANS)
        def _(i, part=part):
            for c in fetches(part, i):
                c.start()

    token = lax.broadcasted_iota(jnp.int32, (rows, 1), 0) % HALF
    for part in range(2):
        span, first, count = spans[part], firsts[part], groups[part]
        q = jnp.concatenate(
            [q_ref[pl.ds(part * HALF, HALF), pl.ds(h * HEAD, HEAD)] for h in range(group)], axis=0
        )
        position = span * HALF + token
        start = start_of(position)
        last_start = start_of(span * HALF + HALF - 1)
        highest[...] = jnp.full_like(highest, NEG)

        @pl.loop(0, count)
        def _(g, part=part):
            for i in range(SPANS):
                fetches(part, g * SPANS + i)[0].wait()
            lead = first + g * SPANS
            kk = k_buf[part, pl.ds(pl.multiple_of(g * wide, wide), wide), :]
            scores = lax.dot_general(
                q, kk, (((1,), (1,)), ((), ())), preferred_element_type=jnp.float32
            )
            inside = jnp.logical_and(lead * HALF >= last_start, lead + SPANS <= span)

            @pl.when(inside)
            def _():
                all_scores[g] = scores
                highest[...] = jnp.maximum(highest[...], scores)

            @pl.when(jnp.logical_not(inside))
            def _():
                place = lead * HALF + lax.broadcasted_iota(jnp.int32, (1, wide), 1)
                allowed = jnp.logical_and(place >= start, place <= position)
                masked = jnp.where(allowed, scores, NEG)
                all_scores[g] = masked
                highest[...] = jnp.maximum(highest[...], masked)

        top = jnp.max(highest[...], axis=1, keepdims=True) * factor
        total[...] = jnp.zeros_like(total)
        acc[...] = jnp.zeros_like(acc)

        @pl.loop(0, count)
        def _(g, part=part):
            for i in range(SPANS):
                fetches(part, g * SPANS + i)[1].wait()
            weights = jnp.exp2(all_scores[g] * factor - top)
            partial = weights[:, :HEAD]
            for i in range(1, wide // HEAD):
                partial = partial + weights[:, i * HEAD : (i + 1) * HEAD]
            total[...] += partial
            acc[...] += jnp.dot(
                weights.astype(jnp.bfloat16),
                v_buf[part, pl.ds(pl.multiple_of(g * wide, wide), wide), :],
                preferred_element_type=jnp.float32,
            )

        done = (acc[...] / jnp.sum(total[...], axis=1, keepdims=True)).astype(jnp.bfloat16)
        for h in range(group):
            out_ref[pl.ds(part * HALF, HALF), pl.ds(h * HEAD, HEAD)] = done[h * HALF : (h + 1) * HALF]


def shards(hidden_x, norm_gain, key_projection, value_projection, queries, span_pair, doc_lengths):
    rows, width = hidden_x.shape
    vmem, smem, anywhere = (
        pl.BlockSpec(memory_space=pltpu.VMEM),
        pl.BlockSpec(memory_space=pltpu.SMEM),
        pl.BlockSpec(memory_space=pl.ANY),
    )
    bf16 = jnp.bfloat16
    exponents = np.arange(HEAD // 2, dtype=np.float32) * np.float32(2.0 / HEAD)
    frequency = np.power(np.float64(ROPE_BASE), -exponents.astype(np.float64)).astype(np.float32)
    frequency = jnp.asarray(np.concatenate([frequency, frequency])[None])
    dma = pltpu.SemaphoreType.DMA
    keys, values, where = pl.pallas_call(
        project_kernel,
        out_shape=(
            jax.ShapeDtypeStruct((NCTX, rows, HEAD), bf16),
            jax.ShapeDtypeStruct((NCTX, rows, HEAD), bf16),
            jax.ShapeDtypeStruct((1, 128), jnp.int32),
        ),
        in_specs=[smem, anywhere, vmem, anywhere, anywhere, vmem],
        out_specs=(anywhere, anywhere, vmem),
        scratch_shapes=[
            pltpu.VMEM((8, rows, width), bf16),
            pltpu.VMEM((8, rows, width), bf16),
            pltpu.VMEM((NCTX, 128 + EXT, HEAD), bf16),
            pltpu.VMEM((NCTX, 128, HEAD), bf16),
            pltpu.VMEM((2, rows, HEAD), jnp.float32),
            pltpu.VMEM((NCTX, rows, HEAD), bf16),
            pltpu.VMEM((NCTX, rows, HEAD), bf16),
            dma((2, CtxGather.N_SEND)),
            dma((2, NCTX)),
            dma((FeatureGather.N_SEND,)),
            dma((8, CHUNKS)),
            dma((2, CtxGather.N_SEND)),
            dma((2, NCTX)),
            dma((3,)),
            dma((2, NCTX // 2)),
        ],
        compiler_params=pltpu.CompilerParams(
            collective_id=0, has_side_effects=True, vmem_limit_bytes=VMEM_LIMIT
        ),
        name="project",
    )(
        span_pair,
        hidden_x,
        norm_gain.reshape(8 * width // HEAD, HEAD),
        key_projection,
        value_projection,
        frequency,
    )
    group = queries.shape[1] // HEAD
    return pl.pallas_call(
        attend_kernel,
        out_shape=jax.ShapeDtypeStruct(queries.shape, bf16),
        in_specs=[smem, smem, smem, vmem, anywhere, anywhere],
        out_specs=vmem,
        scratch_shapes=[
            pltpu.VMEM((2, MOST_SPANS * HALF, HEAD), bf16),
            pltpu.VMEM((2, MOST_SPANS * HALF, HEAD), bf16),
            pltpu.VMEM((MOST_SPANS // SPANS, HALF * group, SPANS * HALF), jnp.float32),
            pltpu.VMEM((HALF * group, SPANS * HALF), jnp.float32),
            pltpu.VMEM((HALF * group, HEAD), jnp.float32),
            pltpu.VMEM((HALF * group, HEAD), jnp.float32),
            dma((2, 2, MOST_SPANS)),
        ],
        compiler_params=pltpu.CompilerParams(vmem_limit_bytes=VMEM_LIMIT),
        name="attend",
    )(span_pair, doc_lengths, where, queries, keys, values)


def solution(mesh):
    placed = (P("ctx", "tp"), P(), P("ctx", "tp"), P("ctx", "tp"), P("ctx", "tp"), P("ctx"), P())
    return jax.shard_map(
        shards, mesh=mesh, in_specs=placed, out_specs=P("ctx", "tp"), check_vma=False
    )
```

time: 690 us -> 114 us (0.17)
  waiting for transfers between devices: 571 us -> 0 us
  Pallas kernels: 0 us -> 113 us
  matrix products: 61.4 us -> 0 us
  other arithmetic: 19.3 us -> 0 us
  blocking collectives: 13.5 us -> 0 us
  between operations: 13.9 us -> 0.66 us
  local copies, waits for them, and re-layouts: 8.41 us -> 0 us
    all_gather x5 -> x0, waiting for transfers between devices: 569 us -> none  [the longest x1 124 us: shards(): whole_x = lax.all_gather(hidden_x, 'tp', axis=1, tiled=True)]
    pallas_call x0 -> x2, Pallas kernels: none -> 113 us  [the longest x1 105 us: shards(): pl.pallas_call(project_kernel, out_shape=(jax.ShapeDtypeStruct((NCTX, row...]
    dot_general x34 -> x0, matrix products: 61.4 us -> none  [the longest x16 30 us: attend(): jnp.einsum('hrn,nhd->hrd', rounded, heads_of_value, preferred_element_typ...]
    reduce_sum x50 -> x0, other arithmetic: 17 us -> none  [the longest x16 11.7 us: attend(): total_next = total_now * shrink + jnp.sum(exp_scores, axis=2)]
    unnamed x1 -> x0, blocking collectives: 13.5 us -> none
  transfers between devices with their start and end apart: 5 -> 0, of which waited for: 5 -> 0; matrix products, arithmetic and copies ran while one was open for 2% -> 0% of each run, Pallas kernels for 0% -> 0%
where the time goes in v1:
time: 114 us
  Pallas kernels  113 us (99%)
    pallas_call x1, Pallas kernels, shards(): pl.pallas_call(project_kernel, out_shape=(jax.ShapeDtypeStruct((NCTX, row...  105 us
    pallas_call x1, Pallas kernels, shards(): pl.pallas_call(attend_kernel, out_shape=jax.ShapeDtypeStruct(queries.shap...  7.71 us

profile of v1, /device:TPU:1, one launch (start us, length us, event | category | flops | bytes accessed | tf_op | source)
XLA Modules:
  0.0 113.8 jit_solution(12136643127150510686)
XLA Ops:
  0.7 105.4 %project.1 = (bf16[64,128,128]{2,1,0:T(8,128)(2,1)}, bf16[64,128,128]{2,1,0:T(8,128)(2,1)}, s32[1,128]{1,0:T(1,128)}) custom-call(s32[1]{0:T(128)S(6)} %copy.9.pair_ref, bf16[128,1024]{1,0:T(8,128)(2,1)} %x_ref.1, f32[64,128]{1,0:T(8,128)} %bitcast.1, bf16[128,128]{1,0:T(8,128)(2,1)} %wk_ref.1, bf16[128,128]{1,0:T(8,128)(2,1)} %wv_ref.1, ...), custom_call_target="tpu_custom_call" | custom-call | tf_op jit(solution)/shard_map/project/pallas_call | solution.py:521
  106.1 7.7 %attend.1 = bf16[128,1024]{1,0:T(8,128)(2,1)} custom-call(s32[1]{0:T(128)S(6)} %copy.9.pair_ref, s32[12]{0:T(128)} %docs_ref.1, s32[1,128]{1,0:T(1,128)} %get-tuple-element.8.where_ref, bf16[128,1024]{1,0:T(8,128)(2,1)} %q_ref.1, bf16[64,128,128]{2,1,0:T(8,128)(2,1)} %get-tuple-element.9.keys_ref, bf16[64,128,128]{2,1,0:T(8,128)(2,1)} %get-tuple-element.10.values_ref), custom_call_target="tpu_custom_call" | custom-call | tf_op jit(solution)/shard_map/attend/pallas_call | solution.py:560
